TPU v7x, 512 devices: a whole 4x8x8 slice. The times are simulated.
512 devices in a mesh: row: 16 (over y, core), col: 16 (over z_hi, x), smp: 2 (over z_lo).
Axes of the slice: x: 4, y: 8, z: 8 (z_hi: 4, z_lo: 2; z = z_hi * 2 + z_lo), core: 2. Of those that a mesh axis runs over, the one named last changes fastest.
Arguments:
- precision: float32 [8192, 8192], P('row', 'col'), as said below
- residuals: float32 [8192, 1024], P(('col', 'row'), 'smp'), may hold values from -6 to 6
- labels: int32 [8192], replicated, may hold values from 0 to 3
Outputs:
- updated: float32 [8192, 8192], P('row', 'col')
Inputs may be any that keep to these rules, and one draw needn't show every extreme that they name: `precision`: symmetric; diagonal entries from 1.5 to 3.
All inputs are finite; a program needn't handle non-finite values.
Results may differ from a plain program's by a relative error of at most 0.0003.
Values sent between devices are 32-bit elements; how exact they have to be, the bound alone decides.
A program may use at most 64 MiB of HBM per device.

v0:
```python
import jax
import jax.numpy as jnp
from jax import lax
from jax.sharding import PartitionSpec as P

STEP_SIZE = 0.5
PENALTY = 0.04


def from_root(block, axis, owner):
    block = jnp.where(lax.axis_index(axis) == owner, block, jnp.zeros_like(block))
    return lax.psum(block, axis)


def contract(left, right):
    return lax.dot_general(
        left,
        right,
        (((1,), (1,)), ((), ())),
        precision=lax.Precision.HIGHEST,
        preferred_element_type=jnp.float32,
    )


def shards(precision, residuals, labels):
    tile = precision.shape[0]
    row_at = lax.axis_index("row")
    col_at = lax.axis_index("col")
    cols_panel = lax.all_gather(residuals, "row", axis=0, tiled=True)
    rows_panel = from_root(cols_panel, "col", row_at)
    partial_rows = jnp.dot(
        precision, cols_panel, precision=lax.Precision.HIGHEST, preferred_element_type=jnp.float32
    )
    row_block = lax.psum(partial_rows, "col")
    partial_cols = lax.dot_general(
        precision,
        rows_panel,
        (((0,), (0,)), ((), ())),
        precision=lax.Precision.HIGHEST,
        preferred_element_type=jnp.float32,
    )
    col_block = lax.psum(partial_cols, "row")
    partial_gram = contract(row_block, cols_panel) + contract(rows_panel, col_block)
    gram = lax.psum(partial_gram, "smp")
    count = residuals.shape[1] * lax.axis_size("smp")
    on_diagonal = row_at == col_at
    ident = jnp.eye(tile, dtype=jnp.float32) * on_diagonal.astype(jnp.float32)
    diag = jnp.diagonal(precision)
    safe_diag = jnp.where(on_diagonal, diag, jnp.ones_like(diag))
    recip = jnp.where(on_diagonal, 1.0 / safe_diag, jnp.zeros_like(diag))
    gradient = gram / (2.0 * count) - ident * recip[:, None]
    moved = precision - STEP_SIZE * gradient
    shrunk = jnp.sign(moved) * jnp.maximum(jnp.abs(moved) - STEP_SIZE * PENALTY, 0.0)
    row_labels = lax.dynamic_slice_in_dim(labels, row_at * tile, tile, 0)
    col_labels = lax.dynamic_slice_in_dim(labels, col_at * tile, tile, 0)
    same = (row_labels[:, None] == col_labels[None, :]).astype(jnp.float32)
    return ident * moved + (1.0 - ident) * shrunk * same


def solution(mesh):
    return jax.shard_map(
        shards,
        mesh=mesh,
        in_specs=(P("row", "col"), P(("col", "row"), "smp"), P()),
        out_specs=P("row", "col"),
        check_vma=False,
    )
```

profile of v0, /device:TPU:1, one launch (start us, length us, event | category | flops | bytes accessed | tf_op | source)
XLA Modules:
  0.0 437.6 jit_solution(2507983678021946761)
XLA Ops:
  6.5 0.0 all-gather.2.cloned.1.call-start
  6.5 0.7 all-gather.2.cloned.1.call-update
  7.3 0.0 all-reduce.9.cloned.1.call-start
  7.3 0.0 copy-start
  7.3 48.8 %all-gather.2.cloned.1.call-done = f32[512,512]{1,0:T(8,128)} async-done(((f32[32,512]{1,0:T(8,128)}), f32[512,512]{1,0:T(8,128)}) %all-gather.2.cloned.1.call-update) | async-done | bytes 1048592 | tf_op jit(solution)/shard_map/all_gather | solution.py:29
  56.1 0.0 copy-start.1
  56.1 1.1 broadcast_select_fusion
  57.2 0.0 copy-done
  57.2 0.5 copy-done.1
  57.7 2.8 fusion.7
  60.5 0.0 all-reduce.9.cloned.1.call-update
  60.5 0.0 all-reduce.5.cloned.1.call-start
  60.6 176.0 %all-reduce.9.cloned.1.call-done = (f32[512,512]{1,0:T(8,128)}, f32[512,512]{1,0:T(8,128)}) async-done(((f32[512,512]{1,0:T(8,128)}, f32[512,512]{1,0:T(8,128)}), (f32[512,512]{1,0:T(8,128)}, f32[512,512]{1,0:T(8,128)})) %all-reduce.9.cloned.1.call-update) | async-done | bytes 2097168 | tf_op jit(solution)/shard_map/psum | solution.py:34
  236.6 4.1 convolution_bitcast_fusion
  240.6 0.0 all-reduce.5.cloned.1.call-update
  240.7 0.0 all-reduce.7.cloned.1.call-start
  240.7 0.0 copy-start.2
  240.7 4.1 fusion.8
  244.9 120.8 %all-reduce.5.cloned.1.call-done = f32[512,512]{0,1:T(8,128)} async-done(((f32[512,512]{0,1:T(8,128)}), f32[512,512]{0,1:T(8,128)}) %all-reduce.5.cloned.1.call-update) | async-done | bytes 1048592 | tf_op jit(solution)/shard_map/psum | solution.py:42
  365.6 0.0 copy-done.2
  365.6 4.4 convolution_add_fusion
  370.0 0.0 all-reduce.7.cloned.1.call-update
  370.0 4.5 %gather_fusion = f32[512]{0:T(512)S(1)} fusion(f32[512,512]{1,0:T(8,128)S(1)} %copy-done, s32[512]{0:T(512)S(1)} %bitcast.11), kind=kCustom, calls=%fused_computation | custom fusion | bytes 8192 | tf_op jit(solution)/shard_map/jit(diagonal)/cond/branch_0_fun/gather | solution.py:48
  374.6 0.8 fusion.6
  375.4 52.7 %all-reduce.7.cloned.1.call-done = f32[512,512]{1,0:T(8,128)} async-done(((f32[512,512]{1,0:T(8,128)}), f32[512,512]{1,0:T(8,128)}) %all-reduce.7.cloned.1.call-update) | async-done | bytes 1048592 | tf_op jit(solution)/shard_map/psum | solution.py:44
  428.1 3.0 fusion.3
  (2 shorter events, 0.0 us)
Async XLA Ops:
  6.5 49.5 %all-gather.2.cloned.1.call-start = ((), (), s32[]{:S(2)}) async-start(), calls=%async_computation | async-start | bytes 1114112 | tf_op jit(solution)/shard_map/all_gather | solution.py:29
  7.3 229.3 %all-reduce.9.cloned.1.call-start = ((), (), s32[]{:S(2)}) async-start(), calls=%async_computation.3 | async-start | bytes 4194304 | tf_op jit(solution)/shard_map/psum | solution.py:34
  7.3 49.8 %copy-start = (f32[512,512]{1,0:T(8,128)S(1)}, f32[512,512]{1,0:T(8,128)}, u32[]{:S(2)}) copy-start(f32[512,512]{1,0:T(8,128)} %param.3) | copy-start | bytes 3145732
  56.1 1.6 copy-start.1
  60.5 305.1 %all-reduce.5.cloned.1.call-start = ((), (), s32[]{:S(2)}) async-start(), calls=%async_computation.1 | async-start | bytes 2097152 | tf_op jit(solution)/shard_map/psum | solution.py:42
  240.7 187.4 %all-reduce.7.cloned.1.call-start = ((), (), s32[]{:S(2)}) async-start(), calls=%async_computation.2 | async-start | bytes 2097152 | tf_op jit(solution)/shard_map/psum | solution.py:44
  240.7 124.9 %copy-start.2 = (f32[512,512]{1,0:T(8,128)S(1)}, f32[512,512]{1,0:T(8,128)}, u32[]{:S(2)}) copy-start(f32[512,512]{1,0:T(8,128)} %get-tuple-element.6) | copy-start | bytes 3145732
Sparse Core Ops, SparseCore 0:
  9.4 46.5 all-gather.1
  60.6 175.8 all-reduce.8
  240.8 124.8 all-reduce.4
  370.1 57.9 all-reduce.6
where the time goes:
time: 438 us
  waiting for transfers between devices  399 us (91%)
  matrix products  15.4 us (4%)
  between operations  13.2 us (3%)
  local copies, waits for them, and re-layouts  5.9 us (1%)
    psum x1, waiting for transfers between devices, shards(): row_block = lax.psum(partial_rows, 'col')  176 us
    psum x1, waiting for transfers between devices, shards(): col_block = lax.psum(partial_cols, 'row')  121 us
    psum x1, waiting for transfers between devices, shards(): gram = lax.psum(partial_gram, 'smp')  52.7 us
    all_gather x1, waiting for transfers between devices, shards(): cols_panel = lax.all_gather(residuals, 'row', axis=0, tiled=True)  48.8 us
  transfers between devices with their start and end apart: 4, of which 4 were waited for; matrix products, arithmetic and copies ran while one was open for 2% of the time, Pallas kernels for 0%

commit v1 on v0

v1 whole, which is shorter than its diff:
```python
import heapq

import jax
import jax.numpy as jnp
from jax import lax
from jax.experimental import pallas as pl
from jax.experimental.pallas import tpu as pltpu
from jax.sharding import PartitionSpec as P

STEP_SIZE = 0.5
PENALTY = 0.04
NY, NX, NZ = 8, 4, 4
SEMS = 160
MESH = pl.DeviceIdType.MESH
F32, BF16 = jnp.float32, jnp.bfloat16


def split(a):
    high = a.astype(BF16)
    return high, (a - high.astype(F32)).astype(BF16)


def product(a, b, dims):
    (ah, al), (bh, bl) = a, b

    def dot(p, q):
        return lax.dot_general(p, q, (dims, ((), ())), preferred_element_type=F32)

    return dot(ah, bh) + dot(ah, bl) + dot(al, bh)


def kernel(count, om, x, lab, out, XJ, WJ, WI, XI, PT, RX, RC, S, RZ, ZC, OM, SAME, XH, XL, WH, WL, ssem, rsem, lsem):
    row, col, u = lax.axis_index("row"), lax.axis_index("col"), lax.axis_index("smp")
    y, core = row // 2, row % 2
    zh, xx = col // NX, col % NX
    v = 1 - u

    def ring(at, by, size):
        return lax.rem(at + by + size, size)

    up, down = {"row": ring(y, 1, NY) * 2 + core}, {"row": ring(y, -1, NY) * 2 + core}
    mate = {"row": y * 2 + 1 - core}
    east, west = {"col": zh * NX + ring(xx, 1, NX)}, {"col": zh * NX + ring(xx, -1, NX)}
    north, south = {"col": ring(zh, 1, NZ) * NX + xx}, {"col": ring(zh, -1, NZ) * NX + xx}
    peer = {"smp": v}
    mirror = {"row": col, "col": row}
    on_diagonal = row == col

    ids = {}
    sent = []

    def tag(key):
        return ids.setdefault(key, len(ids))

    def describe(key, src, dst, to):
        t = tag(key)
        return pltpu.make_async_remote_copy(
            src_ref=src, dst_ref=dst, send_sem=ssem.at[t], recv_sem=rsem.at[t], device_id=to, device_id_type=MESH
        )

    def send(key, src, dst, to):
        copy = describe(key, src, dst, to)
        copy.start()
        sent.append(copy)

    def take(key, dst, to):
        describe(key, dst, dst, to).wait_recv()

    load_x = pltpu.make_async_copy(x, XJ.at[y, core, u], lsem.at[0])
    load_om = pltpu.make_async_copy(om.at[:, :, u], OM, lsem.at[1])
    load_x.start()
    load_om.start()

    barrier = pltpu.get_barrier_semaphore()
    near = (up, down, mate, east, west, north, south, peer)
    for other in near:
        pl.semaphore_signal(barrier, inc=1, device_id=other, device_id_type=MESH)
    pl.semaphore_wait(barrier, len(near))
    load_x.wait()

    def to_mate(name, key, block):
        t = tag((name, "mate", key))
        copy = pltpu.make_async_remote_copy(
            src_ref=block, dst_ref=block, send_sem=ssem.at[t], recv_sem=rsem.at[tag((name, "mate"))],
            device_id=mate, device_id_type=MESH,
        )
        copy.start()
        sent.append(copy)

    def gather_lines(name, B, start, pace):
        own = B.at[y, core, u]
        send((name, "z0"), own, own, peer)
        send((name, "up", 1), own, own, up)
        send((name, "down", 1), own, own, down)
        to_mate(name, "own", own)
        yield start + pace
        theirs = B.at[y, core, v]
        take((name, "z0"), theirs, peer)
        half = B.at[y, core, v, 0]
        send((name, "up v", 1), half, half, up)
        send((name, "down v", 1), half, half, down)
        to_mate(name, "own v", theirs)
        late = []

        def settle():
            for k, below in late:
                at = ring(y, -k if below else k, NY)
                quarter = B.at[at, core, v, 1]
                take((name, "z", k, below), quarter, peer)
                to_mate(name, ("z", k, below), quarter)
            late.clear()

        for k in range(1, NY // 2):
            yield start + pace * (k + 1)
            for below, way, back in ((True, up, down), (False, down, up)):
                verb = "up" if below else "down"
                block = B.at[ring(y, -k if below else k, NY), core, u]
                take((name, verb, k), block, back)
                if k < NY // 2 - 1:
                    send((name, verb, k + 1), block, block, way)
                else:
                    piece = block.at[0 if below else 1]
                    send((name, verb, k + 1), piece, piece, way)
                piece = block.at[1]
                send((name, "z", k, below), piece, piece, peer)
                to_mate(name, ("u", k, below), block)
            for below, way, back in ((True, up, down), (False, down, up)):
                verb = "up" if below else "down"
                block = B.at[ring(y, -k if below else k, NY), core, v, 0]
                take((name, verb + " v", k), block, back)
                if k < NY // 2 - 1:
                    send((name, verb + " v", k + 1), block, block, way)
                to_mate(name, ("v", k, below), block)
            settle()
            late.extend([(k, True), (k, False)])
        yield start + pace * (NY // 2 + 1)
        far = B.at[ring(y, NY // 2, NY), core, u]
        take((name, "up", NY // 2), far.at[0], down)
        take((name, "down", NY // 2), far.at[1], up)
        send((name, "z far"), far, far, peer)
        to_mate(name, "far", far)
        settle()
        yield start + pace * (NY // 2 + 2)
        far = B.at[ring(y, NY // 2, NY), core, v]
        take((name, "z far"), far, peer)
        to_mate(name, "far v", far)
        yield start + pace * (NY // 2 + 3)
        whole = B.at[:, 1 - core]
        pltpu.make_async_remote_copy(
            src_ref=whole, dst_ref=whole, send_sem=ssem.at[0], recv_sem=rsem.at[tag((name, "mate"))],
            device_id=mate, device_id_type=MESH,
        ).wait_recv()

    def gather_plane(name, B, start, pace):
        def spread(z_to, key):
            block = B.at[z_to, xx]
            send((name, "east", key), block, block, east)
            send((name, "west", key), block, block, west)

        def pass_on(z_to, key):
            block = B.at[z_to, ring(xx, -1, NX)]
            take((name, "east", key), block, west)
            send((name, "east 2", key), block.at[0], block.at[0], east)
            block = B.at[z_to, ring(xx, 1, NX)]
            take((name, "west", key), block, east)
            send((name, "west 2", key), block.at[1], block.at[1], west)

        own = B.at[zh, xx]
        send((name, "north"), own, own, north)
        send((name, "south"), own, own, south)
        spread(zh, 0)
        yield start + pace
        block = B.at[ring(zh, -1, NZ), xx]
        take((name, "north"), block, south)
        send((name, "north 2"), block.at[0], block.at[0], north)
        spread(ring(zh, -1, NZ), 1)
        block = B.at[ring(zh, 1, NZ), xx]
        take((name, "south"), block, north)
        send((name, "south 2"), block.at[1], block.at[1], south)
        spread(ring(zh, 1, NZ), 2)
        yield start + pace
        pass_on(zh, 0)
        yield start + pace * 2
        far = B.at[ring(zh, 2, NZ), xx]
        take((name, "north 2"), far.at[0], south)
        take((name, "south 2"), far.at[1], north)
        spread(ring(zh, 2, NZ), 3)
        yield start + pace * 2
        pass_on(ring(zh, -1, NZ), 1)
        yield start + pace * 2.5
        pass_on(ring(zh, 1, NZ), 2)
        yield start + pace * 3
        pass_on(ring(zh, 2, NZ), 3)

    def finish_plane(name, B):
        for key, by in ((0, 0), (1, -1), (2, 1), (3, 2)):
            block = B.at[ring(zh, by, NZ), ring(xx, 2, NX)]
            take((name, "east 2", key), block.at[0], west)
            take((name, "west 2", key), block.at[1], east)

    def run(*phases):
        heap = []
        for n, phase in enumerate(phases):
            heap.append((-1.0, n, phase))
        heapq.heapify(heap)
        while heap:
            _, n, phase = heapq.heappop(heap)
            when = next(phase, None)
            if when is not None:
                heapq.heappush(heap, (when, n, phase))

    phase = gather_lines("X", XJ, 0, 1)
    next(phase)
    classes = lax.broadcasted_iota(jnp.int32, (8, 512), 0)
    ones = (lab[row] == classes).astype(BF16), (lab[col] == classes).astype(BF16)
    same = lax.dot_general(ones[0], ones[1], (((0,), (0,)), ((), ())), preferred_element_type=F32)
    SAME[...] = same.reshape(SAME.shape)
    for _ in phase:
        pass

    load_om.wait()
    om_parts = split(OM[...].reshape(256, 512))
    x2 = ring(xx, 2, NX)
    xe, xw = ring(xx, 1, NX), ring(xx, -1, NX)
    z2 = ring(zh, 2, NZ)
    zn, zs = ring(zh, 1, NZ), ring(zh, -1, NZ)
    low, high = pl.ds(0, 2), pl.ds(2, 2)
    for q in range(2):
        x_parts = split(XJ[:, :, q].reshape(512, 512))
        XH[q], XL[q] = x_parts
        PT[:, :, q] = product(om_parts, x_parts, ((1,), (0,))).reshape(NZ, NX, 16, 512)
        send(("rs far e", q), PT.at[low, x2, q], RX.at[0, q], east)
        send(("rs far w", q), PT.at[high, x2, q], RX.at[1, q], west)
        send(("rs now e", q), PT.at[high, xe, q], RC.at[0, q, high], east)
        send(("rs now w", q), PT.at[low, xw, q], RC.at[1, q, low], west)
    for q in range(2):
        take(("rs far e", q), RX.at[0, q], west)
        PT[low, xe, q] += RX[0, q]
        send(("rs e", q), PT.at[low, xe, q], RC.at[0, q, low], east)
        take(("rs far w", q), RX.at[1, q], east)
        PT[high, xw, q] += RX[1, q]
        send(("rs w", q), PT.at[high, xw, q], RC.at[1, q, high], west)
    top, bottom = pl.ds(0, 8), pl.ds(8, 8)
    for q in range(2):
        take(("rs now e", q), RC.at[0, q, high], west)
        take(("rs now w", q), RC.at[1, q, low], east)
        take(("rs e", q), RC.at[0, q, low], west)
        take(("rs w", q), RC.at[1, q, high], east)
        S[q] = PT[:, xx, q] + RC[0, q] + RC[1, q]
        send(("rz far n", q), S.at[q, z2, top], RZ.at[0, q], north)
        send(("rz far s", q), S.at[q, z2, bottom], RZ.at[1, q], south)
        send(("rz now n", q), S.at[q, zn, bottom], ZC.at[0, q, bottom], north)
        send(("rz now s", q), S.at[q, zs, top], ZC.at[1, q, top], south)
    for q in range(2):
        take(("rz far n", q), RZ.at[0, q], south)
        S[q, zn, top] += RZ[0, q]
        send(("rz n", q), S.at[q, zn, top], ZC.at[0, q, top], north)
        take(("rz far s", q), RZ.at[1, q], north)
        S[q, zs, bottom] += RZ[1, q]
        send(("rz s", q), S.at[q, zs, bottom], ZC.at[1, q, bottom], south)
    for q in range(2):
        take(("rz now n", q), ZC.at[0, q, bottom], south)
        take(("rz now s", q), ZC.at[1, q, top], north)
        take(("rz n", q), ZC.at[0, q, top], south)
        take(("rz s", q), ZC.at[1, q, bottom], north)
        WI[zh, xx, q] = S[q, zh] + ZC[0, q] + ZC[1, q]

    w_away = describe(("turn w"), WI.at[zh, xx], WJ.at[col // 2, col % 2, u], mirror)
    x_away = describe(("turn x"), XJ.at[y, core, :, u], XI.at[row // NX, row % NX], mirror)
    w_stay = pltpu.make_async_copy(WI.at[zh, xx], WJ.at[y, core, u], lsem.at[2])
    x_stay = pltpu.make_async_copy(XJ.at[y, core, :, u], XI.at[zh, xx], lsem.at[3])

    @pl.when(jnp.logical_not(on_diagonal))
    def _():
        w_away.start()
        x_away.start()

    @pl.when(on_diagonal)
    def _():
        w_stay.start()
        x_stay.start()

    def lines():
        yield 7
        pl.when(jnp.logical_not(on_diagonal))(lambda: describe(("turn w"), WI.at[zh, xx], WJ.at[y, core, u], mirror).wait())
        pl.when(on_diagonal)(lambda: w_stay.wait())
        yield from gather_lines("W", WJ, 8, 2)

    def plane():
        yield 7.5
        pl.when(jnp.logical_not(on_diagonal))(
            lambda: describe(("turn x"), XJ.at[y, core, :, u], XI.at[zh, xx], mirror).wait()
        )
        pl.when(on_diagonal)(lambda: x_stay.wait())
        yield from gather_plane("XI", XI, 9, 3.5)

    run(gather_plane("WI", WI, 0, 3.5), lines(), plane())
    finish_plane("WI", WI)

    for q in range(2):
        WH[q], WL[q] = split(WJ[:, :, :, q].reshape(512, 512))
    finish_plane("XI", XI)

    scale = STEP_SIZE / (2.0 * count)
    limit = STEP_SIZE * PENALTY
    columns = lax.broadcasted_iota(jnp.int32, (NZ, 16, 512), 2)
    rows = lax.broadcasted_iota(jnp.int32, (NZ, 16, 512), 0) * (NX * 32) + lax.broadcasted_iota(jnp.int32, (NZ, 16, 512), 1)
    for by in (0, 1, -1, 2):
        at = ring(xx, by, NX)
        gram = jnp.zeros((NZ * 16, 512), F32)
        for q in range(2):
            gram += product(split(WI[:, at, q].reshape(NZ * 16, 512)), (XH[q], XL[q]), ((1,), (1,)))
            gram += product(split(XI[:, at, q].reshape(NZ * 16, 512)), (WH[q], WL[q]), ((1,), (1,)))
        old = OM[:, at]
        hit = jnp.logical_and(rows + (at * 32 + u * 16) == columns, on_diagonal)
        inverse = jnp.where(hit, STEP_SIZE / jnp.where(hit, old, 1.0), 0.0)
        moved = old - scale * gram.reshape(NZ, 16, 512) + inverse
        shrunk = (moved - jnp.minimum(jnp.maximum(moved, -limit), limit)) * SAME[:, at, u]
        out[:, at, u] = jnp.where(hit, moved, shrunk)
        send(("out", by), out.at[:, at, u], out.at[:, at, u], peer)
    for by in (0, 1, -1, 2):
        at = ring(xx, by, NX)
        take(("out", by), out.at[:, at, v], peer)
    for copy in sent:
        copy.wait_send()
    assert len(ids) <= SEMS


def shards(precision, residuals, labels):
    rows, samples = residuals.shape
    count = samples * lax.axis_size("smp")
    dma = pltpu.SemaphoreType.DMA
    any_space = pl.BlockSpec(memory_space=pl.ANY)
    vmem = pl.BlockSpec(memory_space=pltpu.VMEM)
    out = pl.pallas_call(
        lambda *refs: kernel(count, *refs),
        out_shape=jax.ShapeDtypeStruct((NZ, NX, 2, 16, 512), F32),
        in_specs=[any_space, any_space, vmem],
        out_specs=vmem,
        scratch_shapes=[
            pltpu.VMEM((NY, 2, 2, 2, 16, 512), F32),
            pltpu.VMEM((NY, 2, 2, 2, 16, 512), F32),
            pltpu.VMEM((NZ, NX, 2, 16, 512), F32),
            pltpu.VMEM((NZ, NX, 2, 16, 512), F32),
            pltpu.VMEM((NZ, NX, 2, 16, 512), F32),
            pltpu.VMEM((2, 2, 2, 16, 512), F32),
            pltpu.VMEM((2, 2, NZ, 16, 512), F32),
            pltpu.VMEM((2, NZ, 16, 512), F32),
            pltpu.VMEM((2, 2, 8, 512), F32),
            pltpu.VMEM((2, 2, 16, 512), F32),
            pltpu.VMEM((NZ, NX, 16, 512), F32),
            pltpu.VMEM((NZ, NX, 2, 16, 512), F32),
            pltpu.VMEM((2, 512, 512), BF16),
            pltpu.VMEM((2, 512, 512), BF16),
            pltpu.VMEM((2, 512, 512), BF16),
            pltpu.VMEM((2, 512, 512), BF16),
            dma((SEMS,)),
            dma((SEMS,)),
            dma((4,)),
        ],
        compiler_params=pltpu.CompilerParams(collective_id=0, has_side_effects=True, vmem_limit_bytes=48 * 2**20),
    )(
        precision.reshape(NZ, NX, 2, 16, 512).reshape(NZ, NX, 2, 16, 512),
        residuals.reshape(2, 16, 512),
        labels.reshape(16, 1, 512),
    )
    return out.reshape(512, 512)


def solution(mesh):
    return jax.shard_map(
        shards,
        mesh=mesh,
        in_specs=(P("row", "col"), P(("col", "row"), "smp"), P()),
        out_specs=P("row", "col"),
        check_vma=False,
    )
```

time: 438 us -> 121 us (0.28)
  waiting for transfers between devices: 399 us -> 0 us
  Pallas kernels: 0 us -> 117 us
  matrix products: 15.4 us -> 0 us
  between operations: 13.2 us -> 0.01 us
    psum x3 -> x0, waiting for transfers between devices: 349 us -> none  [the longest x1 176 us: shards(): row_block = lax.psum(partial_rows, 'col')]
    pallas_call x0 -> x1, Pallas kernels: none -> 117 us  [shards(): pl.pallas_call(lambda *refs: kernel(count, *refs), out_shape=jax.ShapeDty...]
    all_gather x1 -> x0, waiting for transfers between devices: 48.8 us -> none  [shards(): cols_panel = lax.all_gather(residuals, 'row', axis=0, tiled=True)]
    dot_general x4 -> x0, matrix products: 15.4 us -> none  [the longest x2 8.5 us: contract(): lax.dot_general(left, right, (((1,), (1,)), ((), ())), precision=lax.Prec...]
    gather x1 -> x0, local copies, waits for them, and re-layouts: 4.52 us -> none  [shards(): diag = jnp.diagonal(precision)]
  transfers between devices with their start and end apart: 4 -> 0, of which waited for: 4 -> 0; matrix products, arithmetic and copies ran while one was open for 2% -> 0% of each run, Pallas kernels for 0% -> 0%
where the time goes in v1:
time: 121 us; the launch traced here: 120 us
  Pallas kernels  117 us (97%)
  local copies, waits for them, and re-layouts  3.79 us (3%)
    pallas_call x1, Pallas kernels, shards(): pl.pallas_call(lambda *refs: kernel(count, *refs), out_shape=jax.ShapeDty...  117 us
    unnamed x7, local copies, waits for them, and re-layouts  3.79 us

profile of v1, /device:TPU:1, one launch (start us, length us, event | category | flops | bytes accessed | tf_op | source)
XLA Modules:
  0.0 120.4 jit_solution(9093565239236810912)
XLA Ops:
  0.0 0.0 copy-start
  0.0 1.2 %copy-done = f32[512,512]{1,0:T(8,128)S(1)} copy-done((f32[512,512]{1,0:T(8,128)S(1)}, f32[512,512]{1,0:T(8,128)}, u32[]{:S(2)}) %copy-start) | copy-done | bytes 1048600
  1.2 0.0 copy-start.1
  1.2 0.8 copy-done.1
  2.1 0.0 copy-start.2
  2.1 0.8 copy-done.2
  2.8 116.6 %shard_map.37 = f32[4,4,2,16,512]{4,3,2,1,0:T(8,128)S(1)} custom-call(f32[4,4,2,16,512]{4,3,2,1,0:T(8,128)S(1)} %bitcast.5, f32[2,16,512]{2,1,0:T(8,128)S(1)} %bitcast.6, s32[16,1,512]{2,1,0:T(1,128)S(1)} %bitcast.7), custom_call_target="tpu_custom_call" | custom-call | tf_op jit(solution)/shard_map/pallas_call | solution.py:335
  119.5 1.0 copy.5
Async XLA Ops:
  0.0 1.2 %copy-start = (f32[512,512]{1,0:T(8,128)S(1)}, f32[512,512]{1,0:T(8,128)}, u32[]{:S(2)}) copy-start(f32[512,512]{1,0:T(8,128)} %param.3) | copy-start | bytes 3145732
  1.2 0.8 copy-start.1
  2.1 0.8 copy-start.2

commit v2 on v0

v2 whole, which is shorter than its diff:
```python
import heapq

import jax
import jax.numpy as jnp
from jax import lax
from jax.experimental import pallas as pl
from jax.experimental.pallas import tpu as pltpu
from jax.sharding import PartitionSpec as P

STEP_SIZE = 0.5
PENALTY = 0.04
NY, NX, NZ = 8, 4, 4
SEMS = 400
XI_TIMES = (-9.0, -8.0, 0.5, 1.5, 2.0, 5.0, 9.0)
WI_TIMES = (8.0, 8.2, 11.7, 12.0, 13.0, 16.0, 17.5)
MESH = pl.DeviceIdType.MESH
F32, BF16 = jnp.float32, jnp.bfloat16


def split(a):
    high = a.astype(BF16)
    return high, (a - high.astype(F32)).astype(BF16)


def product(a, b, dims):
    (ah, al), (bh, bl) = a, b

    def dot(p, q):
        return lax.dot_general(p, q, (dims, ((), ())), preferred_element_type=F32)

    return dot(ah, bh) + dot(ah, bl) + dot(al, bh)


def line_slot(row, col):
    dz = (col // NX - row // NX + NZ) % NZ
    dx = (col % NX - row % NX + NX) % NX
    pair = (2 - dz + NZ) % NZ
    odd = (dx // 2 + 1 - pair // 2) % 2
    return ((row // 2 + 2 * pair + odd) % NY) * 2 + dx % 2


def plane_slot(block, y, core):
    away = (y - block // 2 + NY) % NY
    pair = away // 2
    dz = (2 - pair + NZ) % NZ
    dx = ((away % 2 + 1 - pair // 2) % 2) * 2 + core
    return ((block // NX + dz) % NZ) * NX + (block % NX + dx) % NX


def kernel(count, om, x, lab, out, XJ, WJ, WI, XI, PT, RX, RC, S, RZ, ZC, OM, SAME, WC, XH, XL, WIH, WIL, XIH, XIL, LAB, ssem, rsem, lsem):
    row, col, u = lax.axis_index("row"), lax.axis_index("col"), lax.axis_index("smp")
    y, core = row // 2, row % 2
    zh, xx = col // NX, col % NX
    v = 1 - u

    def ring(at, by, size):
        return lax.rem(at + by + size, size)

    up, down = {"row": ring(y, 1, NY) * 2 + core}, {"row": ring(y, -1, NY) * 2 + core}
    mate = {"row": y * 2 + 1 - core}
    east, west = {"col": zh * NX + ring(xx, 1, NX)}, {"col": zh * NX + ring(xx, -1, NX)}
    north, south = {"col": ring(zh, 1, NZ) * NX + xx}, {"col": ring(zh, -1, NZ) * NX + xx}
    peer = {"smp": v}
    to_line = {"row": line_slot(row, col), "col": row}
    to_plane = {"row": col, "col": plane_slot(col, y, core)}
    on_diagonal = row == col

    ids = {}
    sent = []

    def describe(key, src, dst, to):
        t = ids.setdefault(key, len(ids))
        return pltpu.make_async_remote_copy(
            src_ref=src, dst_ref=dst, send_sem=ssem.at[t], recv_sem=rsem.at[t], device_id=to, device_id_type=MESH
        )

    def send(key, src, dst, to):
        copy = describe(key, src, dst, to)
        copy.start()
        sent.append(copy)

    def take(key, dst, to):
        assert key in ids
        describe(key, dst, dst, to).wait_recv()

    load_x = pltpu.make_async_copy(x, XJ.at[row, u], lsem.at[0])
    load_om = pltpu.make_async_copy(om, OM, lsem.at[1])
    load_x.start()
    load_om.start()
    load_lab = pltpu.make_async_copy(lab, LAB, lsem.at[2])
    load_lab.start()

    barrier = pltpu.get_barrier_semaphore()
    ends = [{"row": ring(y, by, NY) * 2 + core} for by in (4, 3, -3, 2, -2)]
    near = (to_line, to_plane, *ends, north, south, east, west, up, down, peer, mate)
    for other in near:
        pl.semaphore_signal(barrier, inc=1, device_id=other, device_id_type=MESH)
    pl.semaphore_wait(barrier, len(near))
    load_x.wait()

    def to_mate(name, k, key, block):
        t = ids.setdefault((name, "mate", key), len(ids))
        r = ids.setdefault((name, "mate", k), len(ids))
        copy = pltpu.make_async_remote_copy(
            src_ref=block, dst_ref=block, send_sem=ssem.at[t], recv_sem=rsem.at[r], device_id=mate, device_id_type=MESH
        )
        copy.start()
        sent.append(copy)

    def take_mate(name, k, B, blocks):
        whole = B.at[pl.ds(0, blocks)]
        pltpu.make_async_remote_copy(
            src_ref=whole, dst_ref=whole, send_sem=ssem.at[0], recv_sem=rsem.at[ids[(name, "mate", k)]],
            device_id=mate, device_id_type=MESH,
        ).wait_recv()

    def gather_lines(name, B, place, all_on_y, start, pace):
        last = NY // 2

        def block(by, half, part=None):
            at = B.at[place(ring(y, by, NY)), half]
            return at if part is None else at.at[part]

        own = block(0, u)
        send((name, "z own"), own, own, peer)
        for part in range(2):
            for verb, way in (("up", up), ("down", down)):
                send((name, verb, 1, 0, part), own.at[part], own.at[part], way)
        to_mate(name, 0, "own", own)
        yield start + pace * 0.9
        theirs = block(0, v)
        take((name, "z own"), theirs, peer)
        parts = 2 if all_on_y else 1
        for part in range(parts):
            for verb, way in (("up", up), ("down", down)):
                send((name, verb, 1, 1, part), theirs.at[part], theirs.at[part], way)
        to_mate(name, 0, "own v", theirs)
        late = []

        def settle():
            for k, by in late:
                piece = block(by, v, 1)
                take((name, "z", by), piece, peer)
                to_mate(name, k, ("z", by), piece)
            late.clear()

        units = [(0, 0), (0, 1), (1, 0), (1, 1)][: 2 + parts]
        for k in range(1, last):
            for n, (other, part) in enumerate(units):
                yield start + pace * (k + n * 0.2)
                for verb, way, back, by in (("up", up, down, -k), ("down", down, up, k)):
                    piece = block(by, v if other else u, part)
                    take((name, verb, k, other, part), piece, back)
                    onward = k < last - 1
                    if k == last - 1:
                        onward = (part == (verb == "down")) if all_on_y or not other else False
                    if onward:
                        send((name, verb, k + 1, other, part), piece, piece, way)
                    if not all_on_y and (other, part) == (0, 1):
                        send((name, "z", by), piece, piece, peer)
                    to_mate(name, k, (by, other, part), piece)
            settle()
            if not all_on_y:
                late.extend([(k, -k), (k, k)])
        for other in range(2 if all_on_y else 1):
            yield start + pace * (last + other * 0.3)
            for part, verb, back in ((0, "up", down), (1, "down", up)):
                piece = block(last, v if other else u, part)
                take((name, verb, last, other, part), piece, back)
                if not all_on_y:
                    send((name, "z far", part), piece, piece, peer)
                to_mate(name, last, (other, part), piece)
        if not all_on_y:
            settle()
            yield start + pace * (last + 0.8)
            for part in range(2):
                piece = block(last, v, part)
                take((name, "z far", part), piece, peer)
                to_mate(name, last, ("v", part), piece)

    def gather_plane(name, B, place, times):
        def block(z_by, x_by):
            return B.at[place(ring(zh, z_by, NZ) * NX + ring(xx, x_by, NX))]

        def spread(z_by):
            at = block(z_by, 0)
            for part in range(2):
                send((name, "east", z_by, part), at.at[part], at.at[part], east)
                send((name, "west", z_by, 1 - part), at.at[1 - part], at.at[1 - part], west)

        def pass_on(z_by):
            at = block(z_by, -1)
            take((name, "east", z_by, 0), at.at[0], west)
            send((name, "east 2", z_by), at.at[0], at.at[0], east)
            at = block(z_by, 1)
            take((name, "west", z_by, 1), at.at[1], east)
            send((name, "west 2", z_by), at.at[1], at.at[1], west)

        own = block(0, 0)
        for part in range(2):
            send((name, "north", part), own.at[part], own.at[part], north)
            send((name, "south", 1 - part), own.at[1 - part], own.at[1 - part], south)
        spread(0)
        yield times[0]
        at = block(-1, 0)
        take((name, "north", 0), at.at[0], south)
        send((name, "north 2"), at.at[0], at.at[0], north)
        at = block(1, 0)
        take((name, "south", 1), at.at[1], north)
        send((name, "south 2"), at.at[1], at.at[1], south)
        take((name, "north", 1), block(-1, 0).at[1], south)
        spread(-1)
        take((name, "south", 0), block(1, 0).at[0], north)
        spread(1)
        yield times[1]
        pass_on(0)
        yield times[2]
        far = block(2, 0)
        take((name, "north 2"), far.at[0], south)
        take((name, "south 2"), far.at[1], north)
        spread(2)
        yield times[3]
        pass_on(-1)
        yield times[4]
        pass_on(1)
        yield times[5]
        pass_on(2)
        yield times[6]
        for z_by in (0, -1, 1, 2):
            take((name, "east", z_by, 1), block(z_by, -1).at[1], west)
            take((name, "west", z_by, 0), block(z_by, 1).at[0], east)
            far = block(z_by, 2)
            take((name, "east 2", z_by), far.at[0], west)
            take((name, "west 2", z_by), far.at[1], east)

    def run(*phases):
        heap = [(-1.0, n, phase) for n, phase in enumerate(phases)]
        heapq.heapify(heap)
        while heap:
            _, n, phase = heapq.heappop(heap)
            when = next(phase, None)
            if when is not None:
                heapq.heappush(heap, (when, n, phase))

    def at_x(by, half):
        return XJ.at[ring(y, by, NY) * 2 + core, half]

    own = at_x(0, u)
    send(("X", "z", 0), own, own, peer)
    orders = (1, -1, 2, -2, 3, -3, 4)
    for by in orders:
        send(("X", by), own, own, {"row": ring(y, by, NY) * 2 + core})
    to_mate("X", 0, "own", own)
    load_lab.wait()
    classes = lax.broadcasted_iota(jnp.int32, (8, 512), 0)
    ones = (LAB[row] == classes).astype(BF16), (LAB[col] == classes).astype(BF16)
    same = lax.dot_general(ones[0], ones[1], (((0,), (0,)), ((), ())), preferred_element_type=F32)
    SAME[...] = same.reshape(SAME.shape)
    theirs = at_x(0, v)
    take(("X", "z", 0), theirs, peer)
    send("turn x", XJ.at[row, :, u], XI.at[row], to_plane)
    to_mate("X", 1, "own v", theirs)
    for by in orders:
        piece = at_x(-by, u)
        take(("X", by), piece, up)
        to_mate("X", 0, by, piece)
        send(("X", "z", by), piece, piece, peer)
    take_mate("X", 0, XJ, 4)

    load_om.wait()
    x_parts = split(XJ[:, u].reshape(512, 512))
    XH[u], XL[u] = x_parts[0].reshape(NZ, 128, 512), x_parts[1].reshape(NZ, 128, 512)
    x2 = ring(xx, 2, NX)
    xe, xw = ring(xx, 1, NX), ring(xx, -1, NX)
    z2 = ring(zh, 2, NZ)
    zn, zs = ring(zh, 1, NZ), ring(zh, -1, NZ)
    low, high = pl.ds(0, 2), pl.ds(2, 2)
    for q in range(2):
        om_parts = split(OM[:, :, q].reshape(256, 512))
        PT[:, :, q] = product(om_parts, x_parts, ((1,), (0,))).reshape(NZ, NX, 16, 512)
        send(("rs far e", q), PT.at[low, x2, q], RX.at[0, q], east)
        send(("rs far w", q), PT.at[high, x2, q], RX.at[1, q], west)
        send(("rs now e", q), PT.at[high, xe, q], RC.at[0, q, high], east)
        send(("rs now w", q), PT.at[low, xw, q], RC.at[1, q, low], west)
    for q in range(2):
        take(("rs far e", q), RX.at[0, q], west)
        PT[low, xe, q] += RX[0, q]
        send(("rs e", q), PT.at[low, xe, q], RC.at[0, q, low], east)
        take(("rs far w", q), RX.at[1, q], east)
        PT[high, xw, q] += RX[1, q]
        send(("rs w", q), PT.at[high, xw, q], RC.at[1, q, high], west)
    take("turn x", XI.at[line_slot(row, col)], to_line)
    plane_x = gather_plane("XI", XI, lambda at: line_slot(row, at), XI_TIMES)
    next(plane_x)
    top, bottom = pl.ds(0, 8), pl.ds(8, 8)
    for q in range(2):
        take(("rs now e", q), RC.at[0, q, high], west)
        take(("rs now w", q), RC.at[1, q, low], east)
        take(("rs e", q), RC.at[0, q, low], west)
        take(("rs w", q), RC.at[1, q, high], east)
        S[q] = PT[:, xx, q] + RC[0, q] + RC[1, q]
        send(("rz far n", q), S.at[q, z2, top], RZ.at[0, q], north)
        send(("rz far s", q), S.at[q, z2, bottom], RZ.at[1, q], south)
        send(("rz now n", q), S.at[q, zn, bottom], ZC.at[0, q, bottom], north)
        send(("rz now s", q), S.at[q, zs, top], ZC.at[1, q, top], south)
    next(plane_x)
    for by in orders:
        piece = at_x(-by, v)
        take(("X", "z", by), piece, peer)
        to_mate("X", 1, by, piece)
    for q in range(2):
        take(("rz far n", q), RZ.at[0, q], south)
        S[q, zn, top] += RZ[0, q]
        send(("rz n", q), S.at[q, zn, top], ZC.at[0, q, top], north)
        take(("rz far s", q), RZ.at[1, q], north)
        S[q, zs, bottom] += RZ[1, q]
        send(("rz s", q), S.at[q, zs, bottom], ZC.at[1, q, bottom], south)
    mine = line_slot(row, col)
    arrives = plane_slot(col, y, core)
    for q in range(2):
        take(("rz now n", q), ZC.at[0, q, bottom], south)
        take(("rz now s", q), ZC.at[1, q, top], north)
        take(("rz n", q), ZC.at[0, q, top], south)
        take(("rz s", q), ZC.at[1, q, bottom], north)
        WC[q] = S[q, zh] + ZC[0, q] + ZC[1, q]
        send(("turn w", q), WC.at[q], WJ.at[col, u, q], to_line)
    send("swap", WC.at[v], WI.at[col, u], peer)
    WI[col, u] = WC[u]

    def lines_w():
        yield 7.0
        for q in range(2):
            take(("turn w", q), WJ.at[arrives, u, q], to_plane)
        yield from gather_lines("W", WJ, lambda at: plane_slot(col, at, core), True, 8.0, 3.6)

    scale = STEP_SIZE / (2.0 * count)
    limit = STEP_SIZE * PENALTY
    first = ((y - col // 2 + NY) % NY) // 2
    back = 1 - 2 * (((y - col // 2 + NY) % NY) % 2)

    def group(n):
        pair = ring(first, (0, -1, 1, 2)[n] * back, 4)
        return ring(col // NX + (2 - pair + NZ) % NZ, 0, NZ)

    def finish_group(n):
        g = group(n)
        lanes = pl.ds(pl.multiple_of(g * 128, 128), 128)
        gram = jnp.zeros((256, 128), F32)
        for q in range(2):
            gram += product((WIH[q], WIL[q]), (XH[q, g], XL[q, g]), ((1,), (1,)))
            w_parts = split(WJ[pl.ds(g * NX, NX), q].reshape(128, 512))
            gram += product((XIH[q], XIL[q]), w_parts, ((1,), (1,)))
        old = OM[:, :, u, :, lanes]
        rows = (lax.broadcasted_iota(jnp.int32, (NZ * NX, 16, 128), 0) * 32 + u * 16).reshape(NZ, NX, 16, 128)
        rows = rows + lax.broadcasted_iota(jnp.int32, (NZ, NX, 16, 128), 2)
        columns = lax.broadcasted_iota(jnp.int32, (NZ, NX, 16, 128), 3) + g * 128
        hit = jnp.logical_and(rows == columns, on_diagonal)
        inverse = jnp.where(hit, STEP_SIZE / jnp.where(hit, old, 1.0), 0.0)
        moved = old - scale * gram.reshape(NZ, NX, 16, 128) + inverse
        shrunk = (moved - jnp.minimum(jnp.maximum(moved, -limit), limit)) * SAME[:, :, u, :, lanes]
        out[:, :, u, :, lanes] = jnp.where(hit, moved, shrunk)
        piece = out.at[:, :, u, :, lanes]
        send(("out", n), piece, piece, peer)

    def grams():
        yield 9.5
        for q in range(2):
            XIH[q], XIL[q] = split(XI[:, q].reshape(256, 512))
        take_mate("X", 1, XJ, 4)
        XH[v], XL[v] = [part.reshape(NZ, 128, 512) for part in split(XJ[:, v].reshape(512, 512))]
        yield 17.6
        for q in range(2):
            WIH[q], WIL[q] = split(WI[:, q].reshape(256, 512))
        take_mate("W", 0, WJ, 1)
        take_mate("W", 1, WJ, 2)
        finish_group(0)
        yield 8.0 + 3.6 * 2 + 3.0
        take_mate("W", 2, WJ, 2)
        finish_group(1)
        yield 8.0 + 3.6 * 3 + 3.0
        take_mate("W", 3, WJ, 2)
        finish_group(2)
        yield 8.0 + 3.6 * 4 + 3.0
        take_mate("W", 4, WJ, 1)
        finish_group(3)

    def plane_w():
        yield 3.5
        take("swap", WI.at[col, v], peer)
        yield from gather_plane("WI", WI, lambda at: at, WI_TIMES)

    run(plane_x, plane_w(), lines_w(), grams())
    for n in range(4):
        piece = out.at[:, :, v, :, pl.ds(pl.multiple_of(group(n) * 128, 128), 128)]
        take(("out", n), piece, peer)
    for copy in sent:
        copy.wait_send()
    assert len(ids) <= SEMS


def shards(precision, residuals, labels):
    count = residuals.shape[1] * lax.axis_size("smp")
    dma = pltpu.SemaphoreType.DMA
    far = lambda a: pltpu.with_memory_space_constraint(a, pltpu.HBM)
    hbm = pl.BlockSpec(memory_space=pltpu.HBM)
    vmem = pl.BlockSpec(memory_space=pltpu.VMEM)
    out = pl.pallas_call(
        lambda *refs: kernel(count, *refs),
        out_shape=jax.ShapeDtypeStruct((NZ, NX, 2, 16, 512), F32),
        in_specs=[hbm, hbm, hbm],
        out_specs=vmem,
        scratch_shapes=[
            pltpu.VMEM((16, 2, 2, 16, 512), F32),
            pltpu.VMEM((16, 2, 2, 16, 512), F32),
            pltpu.VMEM((16, 2, 16, 512), F32),
            pltpu.VMEM((16, 2, 16, 512), F32),
            pltpu.VMEM((NZ, NX, 2, 16, 512), F32),
            pltpu.VMEM((2, 2, 2, 16, 512), F32),
            pltpu.VMEM((2, 2, NZ, 16, 512), F32),
            pltpu.VMEM((2, NZ, 16, 512), F32),
            pltpu.VMEM((2, 2, 8, 512), F32),
            pltpu.VMEM((2, 2, 16, 512), F32),
            pltpu.VMEM((NZ, NX, 2, 16, 512), F32),
            pltpu.VMEM((NZ, NX, 2, 16, 512), F32),
            pltpu.VMEM((2, 16, 512), F32),
            pltpu.VMEM((2, NZ, 128, 512), BF16),
            pltpu.VMEM((2, NZ, 128, 512), BF16),
            pltpu.VMEM((2, 256, 512), BF16),
            pltpu.VMEM((2, 256, 512), BF16),
            pltpu.VMEM((2, 256, 512), BF16),
            pltpu.VMEM((2, 256, 512), BF16),
            pltpu.VMEM((16, 1, 512), jnp.int32),
            dma((SEMS,)),
            dma((SEMS,)),
            dma((4,)),
        ],
        compiler_params=pltpu.CompilerParams(collective_id=0, has_side_effects=True, vmem_limit_bytes=48 * 2**20),
    )(
        far(precision.reshape(NZ, NX, 2, 16, 512)),
        far(residuals.reshape(2, 16, 512)),
        far(labels.reshape(16, 1, 512)),
    )
    return out.reshape(512, 512)


def solution(mesh):
    return jax.shard_map(
        shards,
        mesh=mesh,
        in_specs=(P("row", "col"), P(("col", "row"), "smp"), P()),
        out_specs=P("row", "col"),
        check_vma=False,
    )
```

time: 438 us -> 97.4 us (0.22)
  waiting for transfers between devices: 399 us -> 0 us
  Pallas kernels: 0 us -> 95.8 us
  matrix products: 15.4 us -> 0 us
  between operations: 13.2 us -> 0.01 us
  local copies, waits for them, and re-layouts: 5.9 us -> 0.97 us
    psum x3 -> x0, waiting for transfers between devices: 349 us -> none  [the longest x1 176 us: shards(): row_block = lax.psum(partial_rows, 'col')]
    pallas_call x0 -> x1, Pallas kernels: none -> 95.8 us  [shards(): pl.pallas_call(lambda *refs: kernel(count, *refs), out_shape=jax.ShapeDty...]
    all_gather x1 -> x0, waiting for transfers between devices: 48.8 us -> none  [shards(): cols_panel = lax.all_gather(residuals, 'row', axis=0, tiled=True)]
    dot_general x4 -> x0, matrix products: 15.4 us -> none  [the longest x2 8.5 us: contract(): lax.dot_general(left, right, (((1,), (1,)), ((), ())), precision=lax.Prec...]
    gather x1 -> x0, local copies, waits for them, and re-layouts: 4.52 us -> none  [shards(): diag = jnp.diagonal(precision)]
  transfers between devices with their start and end apart: 4 -> 0, of which waited for: 4 -> 0; matrix products, arithmetic and copies ran while one was open for 2% -> 0% of each run, Pallas kernels for 0% -> 0%
where the time goes in v2:
time: 97.4 us; the launch traced here: 96.8 us
  Pallas kernels  95.8 us (98%)
    pallas_call x1, Pallas kernels, shards(): pl.pallas_call(lambda *refs: kernel(count, *refs), out_shape=jax.ShapeDty...  95.8 us

profile of v2, /device:TPU:1, one launch (start us, length us, event | category | flops | bytes accessed | tf_op | source)
XLA Modules:
  0.0 96.8 jit_solution(5648986174245149693)
XLA Ops:
  0.0 95.8 %shard_map.37 = f32[4,4,2,16,512]{4,3,2,1,0:T(8,128)S(1)} custom-call(f32[4,4,2,16,512]{4,3,2,1,0:T(8,128)} %bitcast.5, f32[2,16,512]{2,1,0:T(8,128)} %bitcast.6, s32[16,1,512]{2,1,0:T(1,128)} %bitcast.7), custom_call_target="tpu_custom_call" | custom-call | tf_op jit(solution)/shard_map/pallas_call | solution.py:407
  95.8 1.0 %copy.5 = f32[512,512]{1,0:T(8,128)} copy(f32[512,512]{1,0:T(8,128)S(1)} %bitcast.4) | data formatting | bytes 2097152

commit v3 on v2

--- a/solution.py
+++ b/solution.py
@@ -11,7 +11,7 @@
 PENALTY = 0.04
 NY, NX, NZ = 8, 4, 4
 SEMS = 400
-XI_TIMES = (-9.0, -8.0, 0.5, 1.5, 2.0, 5.0, 9.0)
+XI_TIMES = (-1.0, 1.0, 4.5, 5.0, 5.5, 8.0, 12.0)
 WI_TIMES = (8.0, 8.2, 11.7, 12.0, 13.0, 16.0, 17.5)
 MESH = pl.DeviceIdType.MESH
 F32, BF16 = jnp.float32, jnp.bfloat16
@@ -47,7 +47,7 @@
     return ((block // NX + dz) % NZ) * NX + (block % NX + dx) % NX
 
 
-def kernel(count, om, x, lab, out, XJ, WJ, WI, XI, PT, RX, RC, S, RZ, ZC, OM, SAME, WC, XH, XL, WIH, WIL, XIH, XIL, LAB, ssem, rsem, lsem):
+def kernel(count, om, x, lab, out, XJ, WJ, WI, XI, PT, RX, RC, S, RZ, ZC, OM, SAME, WC, LEAD, XH, XL, WIH, WIL, XIH, XIL, LAB, ssem, rsem, lsem):
     row, col, u = lax.axis_index("row"), lax.axis_index("col"), lax.axis_index("smp")
     y, core = row // 2, row % 2
     zh, xx = col // NX, col % NX
@@ -258,7 +258,6 @@
     SAME[...] = same.reshape(SAME.shape)
     theirs = at_x(0, v)
     take(("X", "z", 0), theirs, peer)
-    send("turn x", XJ.at[row, :, u], XI.at[row], to_plane)
     to_mate("X", 1, "own v", theirs)
     for by in orders:
         piece = at_x(-by, u)
@@ -266,6 +265,7 @@
         to_mate("X", 0, by, piece)
         send(("X", "z", by), piece, piece, peer)
     take_mate("X", 0, XJ, 4)
+    send("turn x", XJ.at[row, :, u], XI.at[row], to_plane)
 
     load_om.wait()
     x_parts = split(XJ[:, u].reshape(512, 512))
@@ -289,9 +289,6 @@
         take(("rs far w", q), RX.at[1, q], east)
         PT[high, xw, q] += RX[1, q]
         send(("rs w", q), PT.at[high, xw, q], RC.at[1, q, high], west)
-    take("turn x", XI.at[line_slot(row, col)], to_line)
-    plane_x = gather_plane("XI", XI, lambda at: line_slot(row, at), XI_TIMES)
-    next(plane_x)
     top, bottom = pl.ds(0, 8), pl.ds(8, 8)
     for q in range(2):
         take(("rs now e", q), RC.at[0, q, high], west)
@@ -303,6 +300,8 @@
         send(("rz far s", q), S.at[q, z2, bottom], RZ.at[1, q], south)
         send(("rz now n", q), S.at[q, zn, bottom], ZC.at[0, q, bottom], north)
         send(("rz now s", q), S.at[q, zs, top], ZC.at[1, q, top], south)
+    take("turn x", XI.at[line_slot(row, col)], to_line)
+    plane_x = gather_plane("XI", XI, lambda at: line_slot(row, at), XI_TIMES)
     next(plane_x)
     for by in orders:
         piece = at_x(-by, v)
@@ -342,12 +341,18 @@
         pair = ring(first, (0, -1, 1, 2)[n] * back, 4)
         return ring(col // NX + (2 - pair + NZ) % NZ, 0, NZ)
 
+    def lead_group(n):
+        g = group(n)
+        gram = jnp.zeros((256, 128), F32)
+        for q in range(2):
+            gram += product((WIH[q], WIL[q]), (XH[q, g], XL[q, g]), ((1,), (1,)))
+        LEAD[...] = gram
+
     def finish_group(n):
         g = group(n)
         lanes = pl.ds(pl.multiple_of(g * 128, 128), 128)
-        gram = jnp.zeros((256, 128), F32)
+        gram = LEAD[...]
         for q in range(2):
-            gram += product((WIH[q], WIL[q]), (XH[q, g], XL[q, g]), ((1,), (1,)))
             w_parts = split(WJ[pl.ds(g * NX, NX), q].reshape(128, 512))
             gram += product((XIH[q], XIL[q]), w_parts, ((1,), (1,)))
         old = OM[:, :, u, :, lanes]
@@ -363,7 +368,7 @@
         send(("out", n), piece, piece, peer)
 
     def grams():
-        yield 9.5
+        yield 12.5
         for q in range(2):
             XIH[q], XIL[q] = split(XI[:, q].reshape(256, 512))
         take_mate("X", 1, XJ, 4)
@@ -371,15 +376,19 @@
         yield 17.6
         for q in range(2):
             WIH[q], WIL[q] = split(WI[:, q].reshape(256, 512))
+        lead_group(0)
         take_mate("W", 0, WJ, 1)
         take_mate("W", 1, WJ, 2)
         finish_group(0)
+        lead_group(1)
         yield 8.0 + 3.6 * 2 + 3.0
         take_mate("W", 2, WJ, 2)
         finish_group(1)
+        lead_group(2)
         yield 8.0 + 3.6 * 3 + 3.0
         take_mate("W", 3, WJ, 2)
         finish_group(2)
+        lead_group(3)
         yield 8.0 + 3.6 * 4 + 3.0
         take_mate("W", 4, WJ, 1)
         finish_group(3)
@@ -423,6 +432,7 @@
             pltpu.VMEM((NZ, NX, 2, 16, 512), F32),
             pltpu.VMEM((NZ, NX, 2, 16, 512), F32),
             pltpu.VMEM((2, 16, 512), F32),
+            pltpu.VMEM((256, 128), F32),
             pltpu.VMEM((2, NZ, 128, 512), BF16),
             pltpu.VMEM((2, NZ, 128, 512), BF16),
             pltpu.VMEM((2, 256, 512), BF16),

time: 97.4 us -> 97 us (level)
  no operation moved by 1% of the time
where the time goes in v3:
time: 97 us; the launch traced here: 96.5 us
  Pallas kernels  95.6 us (99%)
  local copies, waits for them, and re-layouts  0.97 us (1%)
    pallas_call x1, Pallas kernels, shards(): pl.pallas_call(lambda *refs: kernel(count, *refs), out_shape=jax.ShapeDty...  95.6 us

profile of v3, /device:TPU:1, one launch (start us, length us, event | category | flops | bytes accessed | tf_op | source)
XLA Modules:
  0.0 96.5 jit_solution(9059611705686151673)
XLA Ops:
  0.0 95.6 %shard_map.37 = f32[4,4,2,16,512]{4,3,2,1,0:T(8,128)S(1)} custom-call(f32[4,4,2,16,512]{4,3,2,1,0:T(8,128)} %bitcast.5, f32[2,16,512]{2,1,0:T(8,128)} %bitcast.6, s32[16,1,512]{2,1,0:T(1,128)} %bitcast.7), custom_call_target="tpu_custom_call" | custom-call | tf_op jit(solution)/shard_map/pallas_call | solution.py:416
  95.6 1.0 %copy.5 = f32[512,512]{1,0:T(8,128)} copy(f32[512,512]{1,0:T(8,128)S(1)} %bitcast.4) | data formatting | bytes 2097152
